TPU v7x, 512 devices: a whole 4x4x16 slice. The times are simulated.
512 devices in a mesh: row: 16 (over z_lo, y), col: 32 (over z_hi, x, core).
Axes of the slice: x: 4, y: 4, z: 16 (z_hi: 4, z_lo: 4; z = z_hi * 4 + z_lo), core: 2. Of those that a mesh axis runs over, the one named last changes fastest.
Arguments:
- coupling: bfloat16 [512, 1024, 512], P(('row', 'col')), may hold values from -0.25 to 0.25
- kinv: bfloat16 [512, 512, 512], P(('row', 'col')), as said below
- counts: int32 [512], P(('row', 'col')), may hold values from 4 to 8, as said below
- granules: int32 [512, 8], P(('row', 'col')), may hold values from 0 to 127, as said below
- hessian: bfloat16 [16, 1024, 16384], P(None, 'col', 'row'), as said below
- reg: float32 [16384], P('row'), may hold values from 32 to 96
Outputs:
- trailing: float32 [16, 1024, 16384], P(None, 'col', 'row')
Inputs may be any that keep to these rules, and one draw needn't show every extreme that they name: `counts`: each block couples to between half of 8 and 8 index blocks; some block couples to 8, some to 4. `granules`: row k lists 8 distinct index blocks, all in band k // 32, that is numbers band * 8 to band * 8 + 7. Each kinv[k] is symmetric positive definite. Reshaped to [16384, 16384], hessian is symmetric.
All inputs are finite; a program needn't handle non-finite values.
Results may differ from a plain program's by a relative error of at most 0.00035.
Values sent between devices are 32-bit elements; how exact they have to be, the bound alone decides.
A program may use at most 64 MiB of HBM per device.

v0:
```python
import jax
import jax.numpy as jnp
from jax import lax
from jax.sharding import PartitionSpec as P

PW = 512


def from_root(shard, axis, root):
    mine = lax.axis_index(axis) == root
    return lax.psum(jnp.where(mine, shard, jnp.zeros_like(shard)), axis)


def block_contribution(coupling_rows, kinv_block, count_live, granule_local, granule_count):
    band_width = coupling_rows.shape[0]
    order = coupling_rows.shape[1]
    granule_size = band_width // granule_count
    products = jnp.dot(coupling_rows, kinv_block, preferred_element_type=jnp.float32).astype(
        jnp.bfloat16
    )
    slots = lax.iota(jnp.int32, granule_count)
    placed = (granule_local[None, :] == slots[:, None]) & (slots[None, :] < count_live)
    selector = placed.astype(jnp.bfloat16)
    stacked = jnp.stack([coupling_rows, products]).reshape(2, granule_count, granule_size, order)
    embedded = jnp.einsum("ua,sagn->sugn", selector, stacked, preferred_element_type=jnp.float32)
    embedded = embedded.astype(jnp.bfloat16).reshape(2, band_width, order)
    return lax.dot_general(
        embedded[0], embedded[1], (((1,), (1,)), ((), ())), preferred_element_type=jnp.float32
    )


def local(coupling, kinv, counts, granules, hessian, reg):
    row_index = lax.axis_index("row")
    col_index = lax.axis_index("col")
    band_count = hessian.shape[0]
    col_width = hessian.shape[1]
    band_width = hessian.shape[2]
    granule_count = granules.shape[1]
    local_granules = granules[0] - row_index * granule_count
    addition = block_contribution(coupling[0], kinv[0], counts[0], local_granules, granule_count)
    whole_band = lax.psum(addition, "col")
    share = lax.dynamic_slice_in_dim(whole_band, col_index * col_width, col_width, 0)
    offsets = lax.iota(jnp.int32, band_width)
    local_rows = lax.iota(jnp.int32, col_width)
    on_diagonal = offsets[None, :] == col_index * col_width + local_rows[:, None]
    share = share + jnp.where(on_diagonal, reg[None, :], 0.0)
    band_ids = lax.iota(jnp.int32, band_count)
    schur = hessian.astype(jnp.float32) + jnp.where(
        (band_ids == row_index)[:, None, None], share[None], 0.0
    )
    panel_all = lax.all_gather(schur[0], "col", axis=0, tiled=True)
    panel_rows = panel_all[:PW]
    pivot = from_root(panel_rows[:, :PW], "row", 0)
    lower = jnp.linalg.cholesky(pivot)
    factor_upper = jax.scipy.linalg.solve_triangular(lower, panel_rows, lower=True)
    own_columns = lax.dynamic_slice_in_dim(factor_upper, col_index * col_width, col_width, 1)
    gathered = lax.all_gather(own_columns, "row", axis=1, tiled=True)
    update = lax.dot_general(
        gathered,
        factor_upper,
        (((0,), (0,)), ((), ())),
        precision=lax.Precision.HIGHEST,
        preferred_element_type=jnp.float32,
    )
    update = update.reshape(band_count, col_width, band_width)
    global_rows = band_ids[:, None] * band_width + col_index * col_width + local_rows[None, :]
    global_cols = row_index * band_width + offsets
    keep = (global_rows[:, :, None] >= PW) & (global_cols[None, None, :] >= PW)
    return jnp.where(keep, schur - update, 0.0)


def solution(mesh):
    return jax.shard_map(
        local,
        mesh=mesh,
        in_specs=(
            P(("row", "col"), None, None),
            P(("row", "col"), None, None),
            P(("row", "col")),
            P(("row", "col"), None),
            P(None, "col", "row"),
            P("row"),
        ),
        out_specs=P(None, "col", "row"),
        check_vma=False,
    )
```

profile of v0, /device:TPU:2, one launch (start us, length us, event | category | flops | bytes accessed | tf_op | source)
XLA Modules:
  0.0 931.3 jit_solution(10540804551755899033)
XLA Ops:
  6.5 1.0 copy-done
  7.6 2.0 convolution_convert_fusion
  9.6 0.6 copy.38
  10.2 0.6 copy.37
  11.5 0.7 convert_bitcast_fusion
  12.2 0.1 fusion.52
  12.4 0.3 copy.40
  12.7 0.3 copy.39
  13.0 3.3 fusion.53
  16.4 378.9 %all-reduce.4.cloned.1.call-done = f32[1024,1024]{1,0:T(8,128)} async-done(((f32[1024,1024]{1,0:T(8,128)}), f32[1024,1024]{1,0:T(8,128)}) %all-reduce.4.cloned.1.call-update) | async-done | bytes 4194320 | tf_op jit(solution)/shard_map/psum | solution.py:41
  395.3 1.0 select_add_fusion.1
  396.3 0.4 select_add_fusion
  396.7 0.8 copy.41
  397.5 104.4 %all-gather.6.cloned.1.call-done = f32[1,1024,1024]{2,0,1:T(1,128)} async-done(((f32[1,32,1024]{2,0,1:T(1,128)}), f32[1,1024,1024]{2,0,1:T(1,128)}) %all-gather.6.cloned.1.call-update) | async-done | bytes 4194320 | tf_op jit(solution)/shard_map/all_gather | solution.py:51
  502.0 10.9 %copy.42 = f32[1,1024,1024]{1,2,0:T(8,128)} copy(f32[1,1024,1024]{2,0,1:T(1,128)} %all-gather.6.cloned.1.call-done) | data formatting | bytes 8388608 | tf_op jit(solution)/shard_map/all_gather | solution.py:51
  512.9 2.3 slice_select_fusion
  515.2 0.2 all-gather.4.cloned.1.call-start
  515.5 3.6 fusion.51
  519.1 164.7 %all-reduce.6.cloned.1.call-done = f32[512,512]{0,1:T(8,128)} async-done(((f32[512,512]{0,1:T(8,128)}), f32[512,512]{0,1:T(8,128)}) %all-reduce.6.cloned.1.call-update) | async-done | bytes 1048592 | tf_op jit(solution)/shard_map/psum | solution.py:11
  683.8 1.6 copy.43
  685.4 0.2 fusion.18
  685.7 1.0 copy-done.4
  686.6 11.7 %cholesky.103 = f32[128,128]{1,0:T(8,128)S(1)} custom-call(f32[128,128]{1,0:T(8,128)S(1)} %cholesky.263), custom_call_target="Cholesky" | custom-call | tf_op jit(solution)/shard_map/jit(cholesky)/cholesky | solution.py:54
  698.4 9.8 %custom-call.31 = f32[1,128,128]{1,2,0:T(8,128)S(1)} custom-call(f32[1,128,128]{2,1,0:T(8,128)S(1)} %get-tuple-element.46), custom_call_target="InvertDiagBlocksLowerTriangular" | custom-call | tf_op jit(solution)/shard_map/jit(cholesky)/cholesky | solution.py:54
  708.2 1.2 fusion.27
  709.5 1.3 convolution_subtract_fusion.2
  710.7 11.7 %cholesky.215 = f32[128,128]{1,0:T(8,128)S(1)} custom-call(f32[128,128]{1,0:T(8,128)S(1)} %cholesky.267), custom_call_target="Cholesky" | custom-call | tf_op jit(solution)/shard_map/jit(cholesky)/cholesky | solution.py:54
  723.2 9.8 %custom-call.32 = f32[1,128,128]{1,2,0:T(8,128)S(1)} custom-call(f32[1,128,128]{2,1,0:T(8,128)S(1)} %get-tuple-element.44), custom_call_target="InvertDiagBlocksLowerTriangular" | custom-call | tf_op jit(solution)/shard_map/jit(cholesky)/cholesky | solution.py:54
  733.2 0.3 convolution_dynamic-update-slice_fusion
  733.5 1.5 convolution_subtract_fusion.3
  735.0 11.7 %cholesky.236 = f32[128,128]{1,0:T(8,128)S(1)} custom-call(f32[128,128]{1,0:T(8,128)S(1)} %cholesky.272), custom_call_target="Cholesky" | custom-call | tf_op jit(solution)/shard_map/jit(cholesky)/cholesky | solution.py:54
  746.9 9.8 %custom-call.33 = f32[1,128,128]{1,2,0:T(8,128)S(1)} custom-call(f32[1,128,128]{2,1,0:T(8,128)S(1)} %get-tuple-element.42), custom_call_target="InvertDiagBlocksLowerTriangular" | custom-call | tf_op jit(solution)/shard_map/jit(cholesky)/cholesky | solution.py:54
  756.7 0.3 convolution_dynamic-update-slice_fusion.1
  757.0 1.3 convolution_subtract_fusion.4
  758.3 11.9 %cholesky.253 = f32[128,128]{1,0:T(8,128)S(1)} custom-call(f32[128,128]{1,0:T(8,128)S(1)} %convolution_subtract_fusion.4), custom_call_target="Cholesky" | custom-call | tf_op jit(solution)/shard_map/jit(cholesky)/cholesky | solution.py:54
  770.3 0.7 compare_reduce_fusion.1
  771.0 0.6 compare_reduce_fusion
  771.7 0.7 compare_reduce_fusion.2
  775.1 10.8 %while.1 = (s32[]{:T(128)}, f32[512,512]{0,1:T(8,128)S(1)}, s32[4,2]{0,1:T(2,128)S(1)}, f32[4,128,128]{2,1,0:T(8,128)}, s32[]{:T(128)}) while((s32[]{:T(128)}, f32[512,512]{0,1:T(8,128)S(1)}, s32[4,2]{0,1:T(2,128)S(1)}, f32[4,128,128]{2,1,0:T(8,128)}, s32[]{:T(128)}) %tuple.30), condition=%wide.while_cond, body=%wide.while_body.sunk | while | flops 2 | bytes 393829 | solution.py:55
  775.1 0.5 fusion.63
  775.7 1.3 dynamic-slice.7
  777.1 0.6 bitcast_dynamic-update-slice_fusion.2
  777.8 0.5 fusion.63
  778.4 1.3 dynamic-slice.7
  779.8 0.6 bitcast_dynamic-update-slice_fusion.2
  780.6 0.5 fusion.63
  781.1 1.3 dynamic-slice.7
  782.5 0.6 bitcast_dynamic-update-slice_fusion.2
  783.3 0.5 fusion.63
  783.8 1.3 dynamic-slice.7
  785.3 0.6 bitcast_dynamic-update-slice_fusion.2
  785.9 40.1 %custom-call.34 = f32[4,128,128]{1,2,0:T(8,128)S(1)} custom-call(f32[4,128,128]{2,1,0:T(8,128)} %get-tuple-element.12), custom_call_target="InvertDiagBlocksLowerTriangular" | custom-call | tf_op jit(solution)/shard_map/jit(_solve_triangular)/triangular_solve | solution.py:55
  826.0 1.7 fusion.20
  827.7 0.7 convolution_subtract_fusion.1
  828.4 0.6 fusion.35
  829.1 0.8 convolution_subtract_fusion
  829.9 0.6 fusion.33
  830.5 1.1 fusion.12
  831.7 0.6 fusion.32
  832.3 0.1 pad_maximum_fusion
  832.6 0.7 copy.55
  833.5 84.3 %all-gather.4.cloned.1.call-done = f32[512,512]{0,1:T(8,128)} async-done(((f32[512,32]{0,1:T(8,128)}), f32[512,512]{0,1:T(8,128)}) %all-gather.4.cloned.1.call-update) | async-done | bytes 1048592 | tf_op jit(solution)/shard_map/all_gather | solution.py:57
  917.8 4.9 fusion.49
  922.7 1.9 subtract_select_fusion
  (63 shorter events, 2.0 us)
Async XLA Ops:
  6.5 1.0 copy-start
  6.5 388.7 %all-reduce.4.cloned.1.call-start = ((), (), s32[]{:S(2)}) async-start(), calls=%async_computation | async-start | bytes 8388608 | tf_op jit(solution)/shard_map/psum | solution.py:41
  7.6 2.6 copy-start.7
  9.6 1.9 copy-start.9
  16.3 379.0 %copy-start.8 = (f32[1024]{0:T(1024)S(1)}, f32[1024]{0:T(1024)}, u32[]{:S(2)}) copy-start(f32[1024]{0:T(1024)} %param.11) | copy-start | bytes 12292
  16.3 380.0 %copy-start.2 = (bf16[16,32,1024]{2,1,0:T(8,128)(2,1)S(1)}, bf16[16,32,1024]{2,1,0:T(8,128)(2,1)}, u32[]{:S(2)}) copy-start(bf16[16,32,1024]{2,1,0:T(8,128)(2,1)} %param.10) | copy-start | bytes 3145732
  16.3 485.7 %all-gather.6.cloned.1.call-start = ((), (), s32[]{:S(2)}) async-start(), calls=%async_computation.3 | async-start | bytes 4325376 | tf_op jit(solution)/shard_map/all_gather | solution.py:51
  397.5 286.3 %all-reduce.6.cloned.1.call-start = ((), (), s32[]{:S(2)}) async-start(), calls=%async_computation.1 | async-start | bytes 2097152 | tf_op jit(solution)/shard_map/psum | solution.py:11
  515.2 402.5 %all-gather.4.cloned.1.call-start = ((), (), s32[]{:S(2)}) async-start(), calls=%async_computation.2 | async-start | bytes 1114112 | tf_op jit(solution)/shard_map/all_gather | solution.py:57
  683.8 1.7 copy-start.1
  685.7 1.0 copy-start.4
  775.0 52.7 %copy-start.5 = (f32[1,128,1024]{2,0,1:T(1,128)S(1)}, f32[1,128,1024]{2,0,1:T(1,128)}, u32[]{:S(2)}) copy-start(f32[1,128,1024]{2,0,1:T(1,128)} %get-tuple-element.37) | copy-start | bytes 1572868
  828.4 2.1 copy-start.6
  917.7 4.9 copy-start.3
Sparse Core Ops, SparseCore 0:
  16.4 378.8 all-reduce.3
  398.4 103.5 all-gather.5
  515.3 168.3 all-reduce.5
  833.5 84.2 all-gather.3
where the time goes:
time: 935 us; the launch traced here: 931 us
  waiting for transfers between devices  732 us (78%)
  other arithmetic  125 us (13%)
  local copies, waits for them, and re-layouts  33.3 us (4%)
  matrix products  23 us (2%)
  between operations  17.4 us (2%)
    psum x1, waiting for transfers between devices, local(): whole_band = lax.psum(addition, 'col')  379 us
    psum x1, waiting for transfers between devices, from_root(): return lax.psum(jnp.where(mine, shard, jnp.zeros_like(shard)), axis)  165 us
    all_gather x1, waiting for transfers between devices, local(): panel_all = lax.all_gather(schur[0], 'col', axis=0, tiled=True)  104 us
    all_gather x1, waiting for transfers between devices, local(): gathered = lax.all_gather(own_columns, 'row', axis=1, tiled=True)  84.3 us
    another operation x14, other arithmetic, local(): lower = jnp.linalg.cholesky(pivot)  78.6 us
    another operation x4, other arithmetic, local(): jax.scipy.linalg.solve_triangular(lower, panel_rows, lower=True)  40.4 us
  transfers between devices with their start and end apart: 4, of which 4 were waited for; matrix products, arithmetic and copies ran while one was open for 0% of the time, Pallas kernels for 0%

commit v1 on v0

v1 whole, which is shorter than its diff:
```python
import jax
import jax.numpy as jnp
from jax import lax
from jax.experimental import pallas as pl
from jax.experimental.pallas import tpu as pltpu
from jax.sharding import PartitionSpec as P

PW = 512
MESH = pl.DeviceIdType.MESH
VM = pltpu.VMEM
F32 = jnp.float32
BF16 = jnp.bfloat16
HIGH = lax.Precision.HIGHEST


def in_hbm(a):
    return pltpu.with_memory_space_constraint(a, pltpu.HBM)


def embed_kernel(
    counts_ref, granules_ref, reg_hbm, coupling_hbm, kinv_hbm, emb_ref, diag_ref,
    coupling, kinv, reg, product, loads,
):
    row = lax.axis_index("row")
    col = lax.axis_index("col")
    fetches = [
        pltpu.make_async_copy(coupling_hbm, coupling, loads.at[0]),
        pltpu.make_async_copy(kinv_hbm, kinv, loads.at[1]),
        pltpu.make_async_copy(reg_hbm, reg, loads.at[2]),
    ]
    for fetch in fetches:
        fetch.start()
    for fetch in fetches:
        fetch.wait()
    diag_at = lax.broadcasted_iota(jnp.int32, (32, 1024), 0) + col * 32
    lane_at = lax.broadcasted_iota(jnp.int32, (32, 1024), 1)
    diag_ref[...] = jnp.where(diag_at == lane_at, reg[...], 0.0)
    product[...] = jnp.dot(coupling[...], kinv[...], preferred_element_type=F32).astype(BF16)
    m, n = 128, 512
    for u in range(8):
        slot, live = jnp.int32(0), jnp.int32(0)
        for slot_of in range(8):
            here = (granules_ref[0, slot_of] == row * 8 + u) & (slot_of < counts_ref[0])
            slot = jnp.where(here, slot_of, slot)
            live = jnp.where(here, 1, live)
        block = pl.ds(pl.multiple_of(slot * m, m), m)
        shown = jnp.full((m, n), live, jnp.int32) > 0
        for which, whole in enumerate((coupling, product)):
            emb_ref[which, u * m:(u + 1) * m, :] = jnp.where(shown, whole[block, :], jnp.zeros((m, n), BF16))


def embed(coupling, kinv, counts, granules, reg):
    smem, vmem, hbm = (pl.BlockSpec(memory_space=s) for s in (pltpu.SMEM, pltpu.VMEM, pltpu.HBM))
    return pl.pallas_call(
        embed_kernel,
        name="embed",
        out_shape=(
            jax.ShapeDtypeStruct((2, 1024, 512), BF16),
            jax.ShapeDtypeStruct((32, 1024), F32),
        ),
        in_specs=[smem, smem, hbm, hbm, hbm],
        out_specs=(vmem, vmem),
        scratch_shapes=[
            VM((1024, 512), BF16), VM((512, 512), BF16), VM((1, 1024), F32), VM((1024, 512), BF16),
            pltpu.SemaphoreType.DMA((3,)),
        ],
        compiler_params=pltpu.CompilerParams(vmem_limit_bytes=32 * 2**20),
    )(counts, granules, in_hbm(reg.reshape(1, 1024)), in_hbm(coupling), in_hbm(kinv))


def dot(a, b):
    return lax.dot_general(a, b, (((1,), (0,)), ((), ())), precision=HIGH, preferred_element_type=F32)


def factor_chunk(k, chunk_ref, out, held, done, gathered):
    m, w = 128, 32
    at = pl.multiple_of(k * m, m)
    tile_at = [pl.multiple_of(((k + o) % 4) * m, m) for o in range(4)]
    gathered[...] = dot(out[:, pl.ds(at, m)].T, out[...])
    out[:, pl.ds(at, m)] = jnp.zeros((out.shape[0], m), F32)
    for o in range(4):
        lanes = pl.ds(tile_at[o], m)
        given = chunk_ref[:, :, :, lanes].reshape(m, m)
        held[o] = jnp.where((k + o) % 4 >= k, given, 0.0) - gathered[:, lanes]
    lane = lax.broadcasted_iota(jnp.int32, (1, m), 1)
    for j in range(4):
        tiles = [[held[o, w * j + 8 * i:w * j + 8 * i + 8, :] for o in range(4)] for i in range(4)]
        for r in range(w):
            i0, sub, here = r // 8, r % 8, lane == w * j + r
            first = i0 + (sub == 7)
            factors = {
                i: jnp.broadcast_to(tiles[i][0][:, w * j + r:w * j + r + 1], (8, m)) for i in range(i0, 4)
            }
            pivot = factors[i0][sub:sub + 1, :]
            top = [t[sub:sub + 1, :] for t in tiles[i0]]
            top[0] = jnp.where(here, 1.0, top[0])
            inverse, root = 1.0 / pivot, jnp.sqrt(pivot)
            scaled = [t * inverse for t in top]
            for o in range(4):
                done[o, r:r + 1, :] = scaled[o] * root
            for i in range(first, 4):
                old = [jnp.where(here, 0.0, tiles[i][0])] + tiles[i][1:]
                tiles[i] = [old[o] - factors[i] * jnp.broadcast_to(scaled[o], (8, m)) for o in range(4)]
        for o in range(4):
            out[pl.ds(at + w * j, w), pl.ds(tile_at[o], m)] = done[o]
        if j < 3:
            turned = done[0].T
            gone = (lane >= w * j) & (lane < w * j + w)
            above = gone & (lane > w * j + lax.broadcasted_iota(jnp.int32, (w, 1), 0))
            wide = jnp.concatenate([jnp.where(above, 0.0, done[0])] + [done[o] for o in (1, 2, 3)], axis=1)
            cuts = (w * (j + 1), w * (j + 2), m) if j < 2 else (w * (j + 1), m)
            for lo, hi in zip(cuts, cuts[1:]):
                change = dot(turned[lo:hi], wide)
                for o in range(4):
                    old = held[o, lo:hi, :]
                    if o == 0:
                        old = jnp.where(gone, 0.0, old)
                    held[o, lo:hi, :] = old - change[:, m * o:m * (o + 1)]
    below = lane <= lax.broadcasted_iota(jnp.int32, (m, 1), 0)
    out[pl.ds(at, m), pl.ds(at, m)] = jnp.where(below, out[pl.ds(at, m), pl.ds(at, m)], 0.0)


CHUNKS = range(4)
ORDER = (2, 1, 3, 0)


def schur_kernel(
    emb_ref, diag_ref, hess_hbm,
    inv_ref, panel_ref, rows_ref, share_ref,
    hess_ref, load,
    part, dp, dr, core_in, core_sum, x_in, x_sum, z_in, piv,
    pc_in, pc_sum, px_in, pz, rc_in, rc_sum, rx_in, rz, ry, spare, held, done, gathered,
    s_core, r_core, s_x, r_x, s_z, r_z,
    s_fz, r_fz, s_fx, r_fx, s_fc, r_fc, s_gs, r_gs, s_gt, r_gt, s_gz, r_gz, s_gy, r_gy,
    s_pc, r_pc, s_px, r_px, s_pz, r_pz, s_rc, r_rc, s_rx, r_rx, s_rz, r_rz, s_ry, r_ry,
    s_vy, r_vy, s_vz, r_vz, s_vx, r_vx, s_vc, r_vc,
):
    row = lax.axis_index("row")
    col = lax.axis_index("col")
    zlo, y = row // 4, row % 4
    z, x, core = col // 8, (col // 2) % 4, col % 2
    other = 1 - core
    n, m = PW, 128
    first = row == 0

    def col_of(zz, xx, cc):
        return zz * 8 + xx * 2 + cc

    def row_of(ll, yy):
        return ll * 4 + yy

    def copy(src, dst, ss, rs, r, c):
        return pltpu.make_async_remote_copy(
            src_ref=src, dst_ref=dst, send_sem=ss, recv_sem=rs,
            device_id=(r, c), device_id_type=MESH,
        )

    def by_x(o):
        return row, col_of(z, (x + o) % 4, core)

    def by_z(e):
        return row, col_of((z + e) % 4, x, core)

    def by_y(o):
        return row_of(zlo, (y + o) % 4), col

    def by_l(o):
        return row_of((zlo + o) % 4, y), col

    pair = (row, col_of(z, x, other))

    def t_core(q):
        return copy(part.at[q, :, other], core_in.at[q], s_core.at[q], r_core.at[q], *pair)

    def t_x(q, o):
        return copy(core_sum.at[q, (x + o) % 4], x_in.at[o - 1, q], s_x.at[q, o - 1], r_x.at[q, o - 1], *by_x(o))

    def t_z(e):
        return copy(x_sum.at[(z + e) % 4], z_in.at[e - 1], s_z.at[e - 1], r_z.at[e - 1], *by_z(e))

    def t_fz(e):
        at = panel_ref.at[z % 2, x, core]
        return copy(at, at, s_fz.at[e - 1], r_fz.at[z % 2], *by_z(e))

    def got_fz(s):
        at = panel_ref.at[s, x, core]
        return copy(at, at, s_fz.at[0], r_fz.at[s], *by_z(1))

    def t_fx(s, o, xx):
        at = panel_ref.at[s, xx, core]
        return copy(at, at, s_fx.at[s, o - 1], r_fx.at[s, o - 1], *by_x(o))

    def t_fc(s, cc):
        at = panel_ref.at[s, :, cc]
        return copy(at, at, s_fc.at[s], r_fc.at[s], *pair)

    def t_gs(o, yy):
        return copy(spare.at[:, yy], rows_ref.at[:, yy], s_gs.at[o - 1], r_gs.at[0], *by_y(o))

    def t_gt(o, ll):
        at = rows_ref.at[ll, y]
        return copy(at, at, s_gt.at[o - 1], r_gt.at[0], *by_l(o))

    def t_gz(o, ll):
        at = rows_ref.at[ll, y]
        return copy(at, at, s_gz.at[o - 1], r_gz.at[o - 1], *by_l(o))

    def t_gy(l, o, yy):
        at = rows_ref.at[l, yy]
        return copy(at, at, s_gy.at[l, o - 1], r_gy.at[l, o - 1], *by_y(o))

    def t_pc(i):
        return copy(dp.at[i, :, other, :, m * i:n], pc_in.at[i, :, :, m * i:n], s_pc.at[i], r_pc.at[i], *pair)

    def t_px(i, o):
        return copy(pc_sum.at[i, (x + o) % 4, :, m * i:n], px_in.at[o - 1, i, :, m * i:n],
                    s_px.at[i, o - 1], r_px.at[i, o - 1], *by_x(o))

    def t_pz(i, e, zz):
        at = pz.at[zz, i, :, m * i:n]
        return copy(at, at, s_pz.at[i, e - 1], r_pz.at[i, e - 1], *by_z(e))

    def t_vy(i, o):
        at = piv.at[i, x, core, :, m * i:n]
        return copy(at, at, s_vy.at[i, o - 1], r_vy.at[i], *by_y(o))

    def t_vz(i, o):
        at = piv.at[i, x, core, :, m * i:n]
        return copy(at, at, s_vz.at[i, o - 1], r_vz.at[i], *by_l(o))

    def t_vx(i, o, xx):
        at = piv.at[i, xx, core, :, m * i:n]
        return copy(at, at, s_vx.at[i, o - 1], r_vx.at[i, o - 1], *by_x(o))

    def t_vc(i, cc):
        at = piv.at[i, :, cc, :, m * i:n]
        return copy(at, at, s_vc.at[i], r_vc.at[i], *pair)

    def t_rc(s):
        return copy(dr.at[s, :, other], rc_in.at[s], s_rc.at[s], r_rc.at[s], *pair)

    def t_rx(s, o):
        return copy(rc_sum.at[s, (x + o) % 4], rx_in.at[o - 1, s], s_rx.at[s, o - 1], r_rx.at[s, o - 1], *by_x(o))

    def t_rz(s, e, zz):
        at = rz.at[zz, s]
        return copy(at, at, s_rz.at[s, e - 1], r_rz.at[s, e - 1], *by_z(e))

    def t_ry(e):
        return copy(rz.at[z, (z + e) % 4], ry.at[e - 1], s_ry.at[e - 1], r_ry.at[e - 1], *by_z(e))

    def outer(p, q):
        return lax.dot_general(p, q, (((1,), (1,)), ((), ())), preferred_element_type=F32)

    fetch = pltpu.make_async_copy(hess_hbm, hess_ref, load)
    fetch.start()
    barrier = pltpu.get_barrier_semaphore()

    def greet(device):
        pl.semaphore_signal(barrier, inc=1, device_id=device, device_id_type=MESH)

    greet(pair)
    for o in (1, 2, 3):
        greet(by_z(o))
        greet(by_x(o))
        greet(by_y(o))
        greet(by_l(o))

    fetch.wait()

    @pl.when(first)
    def _():
        both = outer(emb_ref[0, 0:n], emb_ref[1, 0:n]) + outer(emb_ref[1, 0:n], emb_ref[0, 0:n])
        row_block = lax.broadcasted_iota(jnp.int32, (16, 1, 1), 0)
        held_here = (hess_ref[0, :, 0:n].astype(F32) + diag_ref[:, 0:n])[None]
        both = 0.5 * both.reshape(16, 32, n) + jnp.where(row_block == col, held_here, 0.0)
        dp[...] = both.reshape(4, 4, 2, 16, n)
        dr[0:2] = outer(emb_ref[0, 0:n], emb_ref[1, n:2 * n]).reshape(2, 4, 2, 32, n)
        dr[2:4] = outer(emb_ref[1, n:2 * n], emb_ref[0, 0:n]).reshape(2, 4, 2, 32, n)
        for l in range(4):
            for yy in range(4):
                to = spare if yy else rows_ref
                to[l, yy] = hess_ref[4 * l + yy, :, 0:n].astype(F32)
        for s in (0, 1):
            panel_ref[s, x, core, :, 0:n] = jnp.zeros((32, n), F32)

    @pl.when((row != 0) & (z < 2))
    def _():
        panel_ref[z % 2, x, core] = hess_ref[0].astype(F32)

    def contribute(q, _):
        rows_at = pl.ds(pl.multiple_of(q * 256, 256), 256)
        part[q] = outer(emb_ref[0, rows_at], emb_ref[1]).reshape(4, 2, 32, 2 * n)
        return 0

    lax.fori_loop(0, 4, contribute, 0)
    inv_ref[...] = jnp.zeros((n, n), F32)
    pl.semaphore_wait(barrier, 13)

    @pl.when(first)
    def _():
        for i in CHUNKS:
            t_pc(i).start()
        for s in range(4):
            t_rc(s).start()
        for o in (2, 1, 3):
            t_gs(o, (y + o) % 4).start()

    @pl.when((row != 0) & (z < 2))
    def _():
        for e in (2, 1, 3):
            t_fz(e).start()

    for q in range(4):
        t_core(q).start()

    @pl.when(first)
    def _():
        for o in (3, 2, 1):
            t_gt(o, (zlo + o) % 4).start()
        for i in CHUNKS:
            t_pc(i).wait_recv()
            lanes = slice(m * i, n)
            pc_sum[i, :, :, lanes] = dp[i, :, core, :, lanes] + pc_in[i, :, :, lanes]
            for o in (2, 1, 3):
                t_px(i, o).start()
        for s in range(4):
            t_rc(s).wait_recv()
            rc_sum[s] = dr[s, :, core] + rc_in[s]
            for o in (2, 1, 3):
                t_rx(s, o).start()
        for i in CHUNKS:
            for o in (1, 2, 3):
                t_px(i, o).wait_recv()
            lanes = slice(m * i, n)
            pz[z, i, :, lanes] = (pc_sum[i, x, :, lanes] + px_in[0, i, :, lanes]) + (
                px_in[1, i, :, lanes] + px_in[2, i, :, lanes])
            for e in (2, 1, 3):
                t_pz(i, e, z).start()
        for s in range(4):
            for o in (1, 2, 3):
                t_rx(s, o).wait_recv()
            summed = (rc_sum[s, x] + rx_in[0, s]) + (rx_in[1, s] + rx_in[2, s])
            if s < 2:
                summed = summed + jnp.where(z == s, hess_ref[0, :, n:2 * n].astype(F32), 0.0)
            rz[z, s] = summed
            if s < 2:
                for e in (2, 1, 3):
                    t_rz(s, e, z).start()
        for e in (2, 1, 3):
            @pl.when((z + e) % 4 >= 2)
            def _(e=e):
                t_ry(e).start()

    def combine(q, _):
        t_core(q).wait_recv()
        core_sum[q] = part[q, :, core] + core_in[q]
        for o in (2, 1, 3):
            t_x(q, o).start()
        return 0

    lax.fori_loop(0, 4, combine, 0)

    @pl.when(first)
    def _():
        for i in CHUNKS:
            for e in (1, 2, 3):
                t_pz(i, e, (z - e) % 4).wait_recv()
            lanes = slice(m * i, n)
            piv[i, x, core, :, lanes] = (pz[0, i, :, lanes] + pz[1, i, :, lanes]) + (
                pz[2, i, :, lanes] + pz[3, i, :, lanes])
            for o in (2, 1, 3):
                t_vy(i, o).start()
            for o in (3, 2, 1):
                t_vz(i, o).start()

    @pl.when((zlo == 0) & (y != 0))
    def _():
        t_gs(1, y).wait_recv()
        for o in (3, 2, 1):
            t_gt(o, (zlo + o) % 4).start()
            t_gz(o, zlo).start()

    for i in CHUNKS:
        @pl.when((zlo == 0) & (y != 0))
        def _(i=i):
            t_vy(i, 1).wait_recv()
            for o in (3, 2, 1):
                t_vz(i, o).start()

        @pl.when(zlo != 0)
        def _(i=i):
            t_vz(i, 1).wait_recv()

        for o in (2, 1, 3):
            t_vx(i, o, x).start()

    @pl.when(first)
    def _():
        for s in (0, 1):
            for e in (1, 2, 3):
                t_rz(s, e, (z - e) % 4).wait_recv()
            panel_ref[s, x, core, :, n:2 * n] = (rz[0, s] + rz[1, s]) + (rz[2, s] + rz[3, s])

        @pl.when(z >= 2)
        def _():
            for e in (1, 2, 3):
                t_ry(e).wait_recv()
            rows_ref[0, 0] = rows_ref[0, 0] + ((rz[z, z] + ry[0]) + (ry[1] + ry[2]))

        for o in (3, 2, 1):
            t_gz(o, zlo).start()

    @pl.when(zlo != 0)
    def _():
        t_gt(1, zlo).wait_recv()
        for o in (1, 2, 3):
            @pl.when((zlo + o) % 4 != 0)
            def _(o=o):
                t_gz(o, zlo).start()

    for s in (0, 1):
        @pl.when((row != 0) & (z != s))
        def _(s=s):
            got_fz(s).wait_recv()
        for o in (2, 1, 3):
            t_fx(s, o, x).start()
    for i in CHUNKS:
        for o in (1, 2, 3):
            t_vx(i, o, (x - o) % 4).wait_recv()
        t_vc(i, core).start()

    def band_z():
        for e in ORDER:
            q = (z + e) % 4
            for o in (1, 2, 3):
                t_x(q, o).wait_recv()
            x_sum[q] = (core_sum[q, x] + x_in[0, q]) + (x_in[1, q] + x_in[2, q])
            if e:
                t_z(e).start()

    def spread():
        for o in (0, 1, 2, 3):
            l = (zlo - o) % 4
            if o:
                @pl.when(zlo != 0)
                def _(o=o, l=l):
                    t_gz(o, l).wait_recv()
            for v in (2, 1, 3):
                t_gy(l, v, y).start()

    def panel_core():
        for s in (0, 1):
            for o in (1, 2, 3):
                t_fx(s, o, (x - o) % 4).wait_recv()
            t_fc(s, core).start()

    def step(k, _):
        for i in CHUNKS:
            @pl.when(k == i)
            def _(i=i):
                t_vc(i, other).wait_recv()
        factor_chunk(k, piv.at[k], inv_ref, held, done, gathered)
        for kk, work in enumerate((band_z, spread, panel_core)):
            @pl.when(k == kk)
            def _(work=work):
                work()
        return 0

    lax.fori_loop(0, 4, step, 0)
    for e in (1, 2, 3):
        t_z(e).wait_recv()
    share_ref[...] = (x_sum[z] + z_in[0]) + (z_in[1] + z_in[2]) + diag_ref[...]
    for l in range(4):
        for o in (1, 2, 3):
            t_gy(l, o, (y - o) % 4).wait_recv()
    for s in (0, 1):
        t_fc(s, other).wait_recv()

    for e in ORDER:
        t_core(e).wait_send()
        for o in (1, 2, 3):
            t_x(e, o).wait_send()
        if e:
            t_z(e).wait_send()
    for s in (0, 1):
        for o in (1, 2, 3):
            t_fx(s, o, x).wait_send()
        t_fc(s, core).wait_send()
    for o in (1, 2, 3):
        for l in range(4):
            t_gy(l, o, y).wait_send()

        @pl.when((zlo == 0) | ((zlo + o) % 4 != 0))
        def _(o=o):
            t_gz(o, zlo).wait_send()
    for i in CHUNKS:
        for o in (1, 2, 3):
            t_vx(i, o, x).wait_send()
        t_vc(i, core).wait_send()

    @pl.when(zlo == 0)
    def _():
        for o in (1, 2, 3):
            t_gt(o, (zlo + o) % 4).wait_send()
            for i in CHUNKS:
                t_vz(i, o).wait_send()

    @pl.when((row != 0) & (z < 2))
    def _():
        for e in (1, 2, 3):
            t_fz(e).wait_send()

    @pl.when(first)
    def _():
        for o in (1, 2, 3):
            t_gs(o, (y + o) % 4).wait_send()
            for i in CHUNKS:
                t_px(i, o).wait_send()
                t_pz(i, o, z).wait_send()
                t_vy(i, o).wait_send()
            for s in range(4):
                t_rx(s, o).wait_send()
                if s < 2:
                    t_rz(s, o, z).wait_send()

            @pl.when((z + o) % 4 >= 2)
            def _(o=o):
                t_ry(o).wait_send()
        for i in CHUNKS:
            t_pc(i).wait_send()
        for s in range(4):
            t_rc(s).wait_send()


def schur(embedded, diag, hessian):
    spec = pl.BlockSpec(memory_space=pltpu.VMEM)
    dma = pltpu.SemaphoreType.DMA
    pair = lambda *s: [dma(s), dma(s)]
    return pl.pallas_call(
        schur_kernel,
        name="schur",
        out_shape=(
            jax.ShapeDtypeStruct((512, 512), F32),
            jax.ShapeDtypeStruct((2, 4, 2, 32, 1024), F32),
            jax.ShapeDtypeStruct((4, 4, 32, 512), F32),
            jax.ShapeDtypeStruct((32, 1024), F32),
        ),
        in_specs=[spec, spec, pl.BlockSpec(memory_space=pltpu.HBM)],
        out_specs=(spec,) * 4,
        scratch_shapes=[
            VM((16, 32, 1024), BF16), dma(()),
            VM((4, 4, 2, 32, 1024), F32), VM((4, 4, 2, 16, 512), F32), VM((4, 4, 2, 32, 512), F32),
            VM((4, 4, 32, 1024), F32), VM((4, 4, 32, 1024), F32),
            VM((3, 4, 32, 1024), F32), VM((4, 32, 1024), F32), VM((3, 32, 1024), F32),
            VM((4, 4, 2, 16, 512), F32),
            VM((4, 4, 16, 512), F32), VM((4, 4, 16, 512), F32), VM((3, 4, 16, 512), F32), VM((4, 4, 16, 512), F32),
            VM((4, 4, 32, 512), F32), VM((4, 4, 32, 512), F32), VM((3, 4, 32, 512), F32), VM((4, 4, 32, 512), F32),
            VM((3, 32, 512), F32), VM((4, 4, 32, 512), F32),
            VM((4, 128, 128), F32), VM((4, 32, 128), F32), VM((128, 512), F32),
            *pair(4), *pair(4, 3), *pair(3),
            dma((3,)), dma((2,)), *pair(2, 3), *pair(2),
            dma((3,)), dma((1,)), dma((3,)), dma((1,)), *pair(3), *pair(4, 3),
            *pair(4), *pair(4, 3), *pair(4, 3), *pair(4), *pair(4, 3), *pair(2, 3), *pair(3),
            dma((4, 3)), dma((4,)), dma((4, 3)), dma((4,)), *pair(4, 3), *pair(4),
        ],
        compiler_params=pltpu.CompilerParams(
            collective_id=0, has_side_effects=True, vmem_limit_bytes=40 * 2**20
        ),
    )(embedded, diag, in_hbm(hessian))


def split(a):
    hi = a.astype(BF16)
    return hi, (a - hi.astype(F32)).astype(BF16)


def dot3(a, b, trans=False):
    dims = (((1,), (1 if trans else 0,)), ((), ()))
    mm = lambda p, q: lax.dot_general(p, q, dims, preferred_element_type=F32)
    (ah, al), (bh, bl) = a, b
    return mm(ah, bh) + (mm(ah, bl) + mm(al, bh))


def apply_kernel(inv_ref, panel_ref, rows_ref, hess_ref, share_ref, out_ref, uh, ul, vh, vl):
    row = lax.axis_index("row")
    col = lax.axis_index("col")
    at = pl.program_id(0)

    @pl.when(at == 0)
    def _():
        inv = split(inv_ref[...])
        for j in range(4):
            h, l = split(dot3(inv, split(panel_ref[:, 256 * j:256 * (j + 1)])))
            uh[:, 256 * j:256 * (j + 1)] = h
            ul[:, 256 * j:256 * (j + 1)] = l
        for j in range(2):
            h, l = split(dot3(split(rows_ref[256 * j:256 * (j + 1), :]), inv, trans=True))
            vh[256 * j:256 * (j + 1), :] = h
            vl[256 * j:256 * (j + 1), :] = l

    rows = pl.ds(pl.multiple_of(at * 128, 128), 128)
    update = dot3((vh[rows, :], vl[rows, :]), (uh[...], ul[...]))
    lane = lax.broadcasted_iota(jnp.int32, (1, 1024), 1)
    for q in range(4):
        band = at * 4 + q
        schur = hess_ref[q].astype(F32) + jnp.where(band == row, share_ref[...], 0.0)
        keep = (band * 1024 + col * 32 >= PW) & (row * 1024 + lane >= PW)
        out_ref[q] = jnp.where(keep, schur - update[32 * q:32 * (q + 1), :], 0.0)


def apply(inv, panel, rows, hessian, share):
    whole = lambda *s: pl.BlockSpec(s, lambda i: (0,) * len(s))
    return pl.pallas_call(
        apply_kernel,
        name="apply",
        grid=(4,),
        out_shape=jax.ShapeDtypeStruct((16, 32, 1024), F32),
        in_specs=[
            whole(512, 512), whole(512, 1024), whole(512, 512),
            pl.BlockSpec((4, 32, 1024), lambda i: (i, 0, 0)), whole(32, 1024),
        ],
        out_specs=pl.BlockSpec((4, 32, 1024), lambda i: (i, 0, 0)),
        scratch_shapes=[VM((512, 1024), BF16), VM((512, 1024), BF16), VM((512, 512), BF16), VM((512, 512), BF16)],
        compiler_params=pltpu.CompilerParams(
            dimension_semantics=("arbitrary",), vmem_limit_bytes=40 * 2**20
        ),
    )(inv, panel, rows, hessian, share)


def local(coupling, kinv, counts, granules, hessian, reg):
    embedded, diag = embed(coupling[0], kinv[0], counts, granules, reg)
    inv, panel, rows, share = schur(embedded, diag, hessian)
    return apply(inv, panel.reshape(512, 1024), rows.reshape(512, 512), hessian, share)


def solution(mesh):
    return jax.shard_map(
        local,
        mesh=mesh,
        in_specs=(
            P(("row", "col"), None, None),
            P(("row", "col"), None, None),
            P(("row", "col")),
            P(("row", "col"), None),
            P(None, "col", "row"),
            P("row"),
        ),
        out_specs=P(None, "col", "row"),
        check_vma=False,
    )
```

time: 935 us -> 125 us (0.13)
  the two profiles are of different devices: /device:TPU:2 before, /device:TPU:1 now
where the time goes in v1:
time: 125 us; the launch traced here: 124 us
  Pallas kernels  123 us (98%)
    pallas_call x1, Pallas kernels, schur(): pl.pallas_call(schur_kernel, name='schur', out_shape=(jax.ShapeDtypeStruc...  114 us
    pallas_call x1, Pallas kernels, apply(): pl.pallas_call(apply_kernel, name='apply', grid=(4,), out_shape=jax.Shape...  6.06 us
    pallas_call x1, Pallas kernels, embed(): pl.pallas_call(embed_kernel, name='embed', out_shape=(jax.ShapeDtypeStruc...  2.77 us

profile of v1, /device:TPU:1, one launch (start us, length us, event | category | flops | bytes accessed | tf_op | source)
XLA Modules:
  0.0 124.4 jit_solution(11718925337095122298)
XLA Ops:
  0.7 0.0 copy-start.1
  0.7 0.6 copy-done.1
  1.3 0.0 copy-start
  1.3 2.8 %embed.1 = (bf16[2,1024,512]{2,1,0:T(8,128)(2,1)S(1)}, f32[32,1024]{1,0:T(8,128)S(1)}) custom-call(s32[1]{0:T(128)S(6)} %copy.7.counts_ref, s32[1,8]{1,0:T(1,128)S(1)} %copy-done.1, f32[1,1024]{1,0:T(1,128)} %bitcast.9, bf16[1024,512]{1,0:T(8,128)(2,1)} %bitcast.7, bf16[512,512]{1,0:T(8,128)(2,1)} %bitcast.8), custom_call_target="tpu_custom_call" | custom-call | tf_op jit(solution)/shard_map/embed/pallas_call | solution.py:54
  4.1 114.3 %schur.1 = (f32[512,512]{1,0:T(8,128)S(1)}, f32[2,4,2,32,1024]{4,3,2,1,0:T(8,128)S(1)}, f32[4,4,32,512]{3,2,1,0:T(8,128)S(1)}, f32[32,1024]{1,0:T(8,128)S(1)}) custom-call(bf16[2,1024,512]{2,1,0:T(8,128)(2,1)S(1)} %get-tuple-element.11.emb_ref, f32[32,1024]{1,0:T(8,128)S(1)} %get-tuple-element.12.diag_ref, bf16[16,32,1024]{2,1,0:T(8,128)(2,1)} %hess_ref.1), custom_call_target="tpu_custom_call" | custom-call | tf_op jit(solution)/shard_map/schur/pallas_call | solution.py:540
  118.4 0.0 copy-done
  118.4 6.1 %apply.1 = f32[16,32,1024]{2,1,0:T(8,128)} custom-call(f32[512,512]{1,0:T(8,128)S(1)} %get-tuple-element.13.inv_ref, f32[512,1024]{1,0:T(8,128)S(1)} %bitcast.5, f32[512,512]{1,0:T(8,128)S(1)} %bitcast.6, bf16[16,32,1024]{2,1,0:T(8,128)(2,1)S(1)} %copy-done, f32[32,1024]{1,0:T(8,128)S(1)} %get-tuple-element.16.share_ref), custom_call_target="tpu_custom_call" | custom-call | tf_op jit(solution)/shard_map/apply/pallas_call | solution.py:614
Async XLA Ops:
  0.7 0.7 copy-start.1
  1.3 117.1 %copy-start = (bf16[16,32,1024]{2,1,0:T(8,128)(2,1)S(1)}, bf16[16,32,1024]{2,1,0:T(8,128)(2,1)}, u32[]{:S(2)}) copy-start(bf16[16,32,1024]{2,1,0:T(8,128)(2,1)} %hess_ref.1) | copy-start | bytes 3145732

commit v2 on v1

--- a/solution.py
+++ b/solution.py
@@ -76,7 +76,13 @@
     m, w = 128, 32
     at = pl.multiple_of(k * m, m)
     tile_at = [pl.multiple_of(((k + o) % 4) * m, m) for o in range(4)]
-    gathered[...] = dot(out[:, pl.ds(at, m)].T, out[...])
+    for before in range(4):
+        @pl.when(k == before)
+        def _(before=before):
+            if before:
+                gathered[...] = dot(out[0:m * before, m * before:m * (before + 1)].T, out[0:m * before, :])
+            else:
+                gathered[...] = jnp.zeros(gathered.shape, F32)
     out[:, pl.ds(at, m)] = jnp.zeros((out.shape[0], m), F32)
     for o in range(4):
         lanes = pl.ds(tile_at[o], m)
@@ -85,22 +91,32 @@
     lane = lax.broadcasted_iota(jnp.int32, (1, m), 1)
     for j in range(4):
         tiles = [[held[o, w * j + 8 * i:w * j + 8 * i + 8, :] for o in range(4)] for i in range(4)]
-        for r in range(w):
-            i0, sub, here = r // 8, r % 8, lane == w * j + r
-            first = i0 + (sub == 7)
-            factors = {
-                i: jnp.broadcast_to(tiles[i][0][:, w * j + r:w * j + r + 1], (8, m)) for i in range(i0, 4)
-            }
-            pivot = factors[i0][sub:sub + 1, :]
+        for r in range(0, w, 2):
+            i0, sub = r // 8, r % 8
+            one, two = lane == w * j + r, lane == w * j + r + 1
+            first = i0 + (sub == 6)
+            f0, f1 = (
+                {i: jnp.broadcast_to(tiles[i][0][:, w * j + c:w * j + c + 1], (8, m)) for i in range(i0, 4)}
+                for c in (r, r + 1)
+            )
+            p, q, s = f0[i0][sub:sub + 1, :], f1[i0][sub:sub + 1, :], f1[i0][sub + 1:sub + 2, :]
+            det = p * s - q * q
+            inverse = jnp.broadcast_to(1.0 / det, (8, m))
             top = [t[sub:sub + 1, :] for t in tiles[i0]]
-            top[0] = jnp.where(here, 1.0, top[0])
-            inverse, root = 1.0 / pivot, jnp.sqrt(pivot)
-            scaled = [t * inverse for t in top]
+            low = [t[sub + 1:sub + 2, :] for t in tiles[i0]]
+            top[0] = jnp.where(one, 1.0, jnp.where(two, 0.0, top[0]))
+            low[0] = jnp.where(two, 1.0, jnp.where(one, 0.0, low[0]))
+            u0 = [s * t - q * l for t, l in zip(top, low)]
+            u1 = [p * l - q * t for t, l in zip(top, low)]
+            root0, root1 = 1.0 / jnp.sqrt(p), 1.0 / jnp.sqrt(p * det)
             for o in range(4):
-                done[o, r:r + 1, :] = scaled[o] * root
+                done[o, r:r + 1, :] = top[o] * root0
+                done[o, r + 1:r + 2, :] = u1[o] * root1
+            b0 = [jnp.broadcast_to(u, (8, m)) for u in u0]
+            b1 = [jnp.broadcast_to(u, (8, m)) for u in u1]
             for i in range(first, 4):
-                old = [jnp.where(here, 0.0, tiles[i][0])] + tiles[i][1:]
-                tiles[i] = [old[o] - factors[i] * jnp.broadcast_to(scaled[o], (8, m)) for o in range(4)]
+                old = [jnp.where(one | two, 0.0, tiles[i][0])] + tiles[i][1:]
+                tiles[i] = [old[o] - inverse * (f0[i] * b0[o] + f1[i] * b1[o]) for o in range(4)]
         for o in range(4):
             out[pl.ds(at + w * j, w), pl.ds(tile_at[o], m)] = done[o]
         if j < 3:
@@ -169,14 +185,14 @@
 
     pair = (row, col_of(z, x, other))
 
-    def t_core(q):
-        return copy(part.at[q, :, other], core_in.at[q], s_core.at[q], r_core.at[q], *pair)
-
-    def t_x(q, o):
-        return copy(core_sum.at[q, (x + o) % 4], x_in.at[o - 1, q], s_x.at[q, o - 1], r_x.at[q, o - 1], *by_x(o))
-
-    def t_z(e):
-        return copy(x_sum.at[(z + e) % 4], z_in.at[e - 1], s_z.at[e - 1], r_z.at[e - 1], *by_z(e))
+    def t_core(q, lo=0):
+        return copy(part.at[q, :, other, :, lo:2 * n], core_in.at[q, :, :, lo:2 * n], s_core.at[q], r_core.at[q], *pair)
+
+    def t_x(q, o, lo=0):
+        return copy(core_sum.at[q, (x + o) % 4, :, lo:2 * n], x_in.at[o - 1, q, :, lo:2 * n], s_x.at[q, o - 1], r_x.at[q, o - 1], *by_x(o))
+
+    def t_z(e, lo=0):
+        return copy(x_sum.at[(z + e) % 4, :, lo:2 * n], z_in.at[e - 1, :, lo:2 * n], s_z.at[e - 1], r_z.at[e - 1], *by_z(e))
 
     def t_fz(e):
         at = panel_ref.at[z % 2, x, core]
@@ -186,12 +202,12 @@
         at = panel_ref.at[s, x, core]
         return copy(at, at, s_fz.at[0], r_fz.at[s], *by_z(1))
 
-    def t_fx(s, o, xx):
-        at = panel_ref.at[s, xx, core]
+    def t_fx(s, o, xx, lo=0):
+        at = panel_ref.at[s, xx, core, :, lo:2 * n]
         return copy(at, at, s_fx.at[s, o - 1], r_fx.at[s, o - 1], *by_x(o))
 
-    def t_fc(s, cc):
-        at = panel_ref.at[s, :, cc]
+    def t_fc(s, cc, lo=0):
+        at = panel_ref.at[s, :, cc, :, lo:2 * n]
         return copy(at, at, s_fc.at[s], r_fc.at[s], *pair)
 
     def t_gs(o, yy):
@@ -281,8 +297,7 @@
             for yy in range(4):
                 to = spare if yy else rows_ref
                 to[l, yy] = hess_ref[4 * l + yy, :, 0:n].astype(F32)
-        for s in (0, 1):
-            panel_ref[s, x, core, :, 0:n] = jnp.zeros((32, n), F32)
+        panel_ref[:, :, :, :, 0:n] = jnp.zeros((2, 4, 2, 32, n), F32)
 
     @pl.when((row != 0) & (z < 2))
     def _():
@@ -311,8 +326,17 @@
         for e in (2, 1, 3):
             t_fz(e).start()
 
-    for q in range(4):
-        t_core(q).start()
+    others = row != 0
+
+    @pl.when(others)
+    def _():
+        for q in range(4):
+            t_core(q).start()
+
+    @pl.when(first)
+    def _():
+        for q in (2, 3):
+            t_core(q, n).start()
 
     @pl.when(first)
     def _():
@@ -359,7 +383,17 @@
             t_x(q, o).start()
         return 0
 
-    lax.fori_loop(0, 4, combine, 0)
+    @pl.when(others)
+    def _():
+        lax.fori_loop(0, 4, combine, 0)
+
+    @pl.when(first)
+    def _():
+        for q in (2, 3):
+            t_core(q, n).wait_recv()
+            core_sum[q, :, :, n:2 * n] = part[q, :, core, :, n:2 * n] + core_in[q, :, :, n:2 * n]
+            for o in (2, 1, 3):
+                t_x(q, o, n).start()
 
     @pl.when(first)
     def _():
@@ -420,24 +454,44 @@
                 t_gz(o, zlo).start()
 
     for s in (0, 1):
-        @pl.when((row != 0) & (z != s))
+        @pl.when(others & (z != s))
         def _(s=s):
             got_fz(s).wait_recv()
-        for o in (2, 1, 3):
-            t_fx(s, o, x).start()
+
+        @pl.when(others)
+        def _(s=s):
+            for o in (2, 1, 3):
+                t_fx(s, o, x).start()
+
+        @pl.when(first)
+        def _(s=s):
+            for o in (2, 1, 3):
+                t_fx(s, o, x, n).start()
     for i in CHUNKS:
         for o in (1, 2, 3):
             t_vx(i, o, (x - o) % 4).wait_recv()
         t_vc(i, core).start()
 
-    def band_z():
+    def band_x(e, lo):
+        q = (z + e) % 4
+        for o in (1, 2, 3):
+            t_x(q, o, lo).wait_recv()
+        to = slice(lo, 2 * n)
+        x_sum[q, :, to] = (core_sum[q, x, :, to] + x_in[0, q, :, to]) + (x_in[1, q, :, to] + x_in[2, q, :, to])
+        if e:
+            t_z(e, lo).start()
+
+    @pl.when(others)
+    def _():
+        for e in (2, 1, 3):
+            band_x(e, 0)
+
+    @pl.when(first)
+    def _():
         for e in ORDER:
-            q = (z + e) % 4
-            for o in (1, 2, 3):
-                t_x(q, o).wait_recv()
-            x_sum[q] = (core_sum[q, x] + x_in[0, q]) + (x_in[1, q] + x_in[2, q])
-            if e:
-                t_z(e).start()
+            @pl.when((z + e) % 4 >= 2)
+            def _(e=e):
+                band_x(e, n)
 
     def spread():
         for o in (0, 1, 2, 3):
@@ -450,10 +504,13 @@
                 t_gy(l, v, y).start()
 
     def panel_core():
-        for s in (0, 1):
-            for o in (1, 2, 3):
-                t_fx(s, o, (x - o) % 4).wait_recv()
-            t_fc(s, core).start()
+        for mine, lo in ((others, 0), (first, n)):
+            @pl.when(mine)
+            def _(lo=lo):
+                for s in (0, 1):
+                    for o in (1, 2, 3):
+                        t_fx(s, o, (x - o) % 4, lo).wait_recv()
+                    t_fc(s, core, lo).start()
 
     def step(k, _):
         for i in CHUNKS:
@@ -461,32 +518,68 @@
             def _(i=i):
                 t_vc(i, other).wait_recv()
         factor_chunk(k, piv.at[k], inv_ref, held, done, gathered)
-        for kk, work in enumerate((band_z, spread, panel_core)):
+        for kk, work in enumerate((spread, panel_core)):
             @pl.when(k == kk)
             def _(work=work):
                 work()
         return 0
 
     lax.fori_loop(0, 4, step, 0)
-    for e in (1, 2, 3):
-        t_z(e).wait_recv()
-    share_ref[...] = (x_sum[z] + z_in[0]) + (z_in[1] + z_in[2]) + diag_ref[...]
     for l in range(4):
         for o in (1, 2, 3):
             t_gy(l, o, (y - o) % 4).wait_recv()
-    for s in (0, 1):
-        t_fc(s, other).wait_recv()
-
-    for e in ORDER:
-        t_core(e).wait_send()
-        for o in (1, 2, 3):
-            t_x(e, o).wait_send()
-        if e:
+    for mine, lo in ((others, 0), (first, n)):
+        @pl.when(mine)
+        def _(lo=lo):
+            for s in (0, 1):
+                t_fc(s, other, lo).wait_recv()
+
+    def share_of(lo):
+        for e in (1, 2, 3):
+            t_z(e, lo).wait_recv()
+        to = slice(lo, 2 * n)
+        share_ref[:, to] = (x_sum[z, :, to] + z_in[0, :, to]) + (z_in[1, :, to] + z_in[2, :, to]) + diag_ref[:, to]
+
+    @pl.when(others)
+    def _():
+        band_x(0, 0)
+        share_of(0)
+
+    @pl.when(first)
+    def _():
+        share_ref[...] = jnp.zeros((32, 2 * n), F32)
+
+        @pl.when(z >= 2)
+        def _():
+            share_of(n)
+
+    @pl.when(others)
+    def _():
+        for q in range(4):
+            t_core(q).wait_send()
+            for o in (1, 2, 3):
+                t_x(q, o).wait_send()
+        for e in (1, 2, 3):
             t_z(e).wait_send()
-    for s in (0, 1):
-        for o in (1, 2, 3):
-            t_fx(s, o, x).wait_send()
-        t_fc(s, core).wait_send()
+
+    @pl.when(first)
+    def _():
+        for q in (2, 3):
+            t_core(q, n).wait_send()
+            for o in (1, 2, 3):
+                t_x(q, o, n).wait_send()
+        for e in (1, 2, 3):
+            @pl.when((z + e) % 4 >= 2)
+            def _(e=e):
+                t_z(e, n).wait_send()
+
+    for mine, lo in ((others, 0), (first, n)):
+        @pl.when(mine)
+        def _(lo=lo):
+            for s in (0, 1):
+                for o in (1, 2, 3):
+                    t_fx(s, o, x, lo).wait_send()
+                t_fc(s, core, lo).wait_send()
     for o in (1, 2, 3):
         for l in range(4):
             t_gy(l, o, y).wait_send()
@@ -589,15 +682,14 @@
 
     @pl.when(at == 0)
     def _():
-        inv = split(inv_ref[...])
-        for j in range(4):
-            h, l = split(dot3(inv, split(panel_ref[:, 256 * j:256 * (j + 1)])))
-            uh[:, 256 * j:256 * (j + 1)] = h
-            ul[:, 256 * j:256 * (j + 1)] = l
-        for j in range(2):
-            h, l = split(dot3(split(rows_ref[256 * j:256 * (j + 1), :]), inv, trans=True))
-            vh[256 * j:256 * (j + 1), :] = h
-            vl[256 * j:256 * (j + 1), :] = l
+        for lo, hi in ((0, 256), (256, 512)):
+            inv = split(inv_ref[lo:hi, 0:hi])
+            for j in range(4):
+                part = slice(256 * j, 256 * (j + 1))
+                uh[lo:hi, part], ul[lo:hi, part] = split(dot3(inv, split(panel_ref[0:hi, part])))
+            for j in range(2):
+                part = slice(256 * j, 256 * (j + 1))
+                vh[part, lo:hi], vl[part, lo:hi] = split(dot3(split(rows_ref[part, 0:hi]), inv, trans=True))
 
     rows = pl.ds(pl.multiple_of(at * 128, 128), 128)
     update = dot3((vh[rows, :], vl[rows, :]), (uh[...], ul[...]))

time: 125 us -> 110 us (0.88)
  the two profiles are of different devices: /device:TPU:1 before, /device:TPU:160 now
where the time goes in v2:
time: 110 us; the launch traced here: 109 us
  Pallas kernels  108 us (98%)
    pallas_call x1, Pallas kernels, schur(): pl.pallas_call(schur_kernel, name='schur', out_shape=(jax.ShapeDtypeStruc...  99.8 us
    pallas_call x1, Pallas kernels, apply(): pl.pallas_call(apply_kernel, name='apply', grid=(4,), out_shape=jax.Shape...  5.49 us
    pallas_call x1, Pallas kernels, embed(): pl.pallas_call(embed_kernel, name='embed', out_shape=(jax.ShapeDtypeStruc...  2.77 us

profile of v2, /device:TPU:160, one launch (start us, length us, event | category | flops | bytes accessed | tf_op | source)
XLA Modules:
  0.0 109.4 jit_solution(13864161095249381718)
XLA Ops:
  0.7 0.0 copy-start.1
  0.7 0.6 copy-done.1
  1.3 0.0 copy-start
  1.3 2.8 %embed.1 = (bf16[2,1024,512]{2,1,0:T(8,128)(2,1)S(1)}, f32[32,1024]{1,0:T(8,128)S(1)}) custom-call(s32[1]{0:T(128)S(6)} %copy.7.counts_ref, s32[1,8]{1,0:T(1,128)S(1)} %copy-done.1, f32[1,1024]{1,0:T(1,128)} %bitcast.9, bf16[1024,512]{1,0:T(8,128)(2,1)} %bitcast.7, bf16[512,512]{1,0:T(8,128)(2,1)} %bitcast.8), custom_call_target="tpu_custom_call" | custom-call | tf_op jit(solution)/shard_map/embed/pallas_call | solution.py:54
  4.1 99.8 %schur.1 = (f32[512,512]{1,0:T(8,128)S(1)}, f32[2,4,2,32,1024]{4,3,2,1,0:T(8,128)S(1)}, f32[4,4,32,512]{3,2,1,0:T(8,128)S(1)}, f32[32,1024]{1,0:T(8,128)S(1)}) custom-call(bf16[2,1024,512]{2,1,0:T(8,128)(2,1)S(1)} %get-tuple-element.11.emb_ref, f32[32,1024]{1,0:T(8,128)S(1)} %get-tuple-element.12.diag_ref, bf16[16,32,1024]{2,1,0:T(8,128)(2,1)} %hess_ref.1), custom_call_target="tpu_custom_call" | custom-call | tf_op jit(solution)/shard_map/schur/pallas_call | solution.py:633
  103.9 0.0 copy-done
  103.9 5.5 %apply.1 = f32[16,32,1024]{2,1,0:T(8,128)} custom-call(f32[512,512]{1,0:T(8,128)S(1)} %get-tuple-element.13.inv_ref, f32[512,1024]{1,0:T(8,128)S(1)} %bitcast.5, f32[512,512]{1,0:T(8,128)S(1)} %bitcast.6, bf16[16,32,1024]{2,1,0:T(8,128)(2,1)S(1)} %copy-done, f32[32,1024]{1,0:T(8,128)S(1)} %get-tuple-element.16.share_ref), custom_call_target="tpu_custom_call" | custom-call | tf_op jit(solution)/shard_map/apply/pallas_call | solution.py:706
Async XLA Ops:
  0.7 0.7 copy-start.1
  1.3 102.6 %copy-start = (bf16[16,32,1024]{2,1,0:T(8,128)(2,1)S(1)}, bf16[16,32,1024]{2,1,0:T(8,128)(2,1)}, u32[]{:S(2)}) copy-start(bf16[16,32,1024]{2,1,0:T(8,128)(2,1)} %hess_ref.1) | copy-start | bytes 3145732

commit v3 on v2

--- a/solution.py
+++ b/solution.py
@@ -142,8 +142,8 @@
 
 def schur_kernel(
     emb_ref, diag_ref, hess_hbm,
-    inv_ref, panel_ref, rows_ref, share_ref,
-    hess_ref, load,
+    uh_ref, ul_ref, vh_ref, vl_ref, share_ref,
+    inv_ref, panel_ref, rows_ref, hess_ref, load,
     part, dp, dr, core_in, core_sum, x_in, x_sum, z_in, piv,
     pc_in, pc_sum, px_in, pz, rc_in, rc_sum, rx_in, rz, ry, spare, held, done, gathered,
     s_core, r_core, s_x, r_x, s_z, r_z,
@@ -330,8 +330,8 @@
 
     @pl.when(others)
     def _():
-        for q in range(4):
-            t_core(q).start()
+        for e in ORDER:
+            t_core((z + e) % 4).start()
 
     @pl.when(first)
     def _():
@@ -376,101 +376,11 @@
             def _(e=e):
                 t_ry(e).start()
 
-    def combine(q, _):
+    def combine(q):
         t_core(q).wait_recv()
         core_sum[q] = part[q, :, core] + core_in[q]
         for o in (2, 1, 3):
             t_x(q, o).start()
-        return 0
-
-    @pl.when(others)
-    def _():
-        lax.fori_loop(0, 4, combine, 0)
-
-    @pl.when(first)
-    def _():
-        for q in (2, 3):
-            t_core(q, n).wait_recv()
-            core_sum[q, :, :, n:2 * n] = part[q, :, core, :, n:2 * n] + core_in[q, :, :, n:2 * n]
-            for o in (2, 1, 3):
-                t_x(q, o, n).start()
-
-    @pl.when(first)
-    def _():
-        for i in CHUNKS:
-            for e in (1, 2, 3):
-                t_pz(i, e, (z - e) % 4).wait_recv()
-            lanes = slice(m * i, n)
-            piv[i, x, core, :, lanes] = (pz[0, i, :, lanes] + pz[1, i, :, lanes]) + (
-                pz[2, i, :, lanes] + pz[3, i, :, lanes])
-            for o in (2, 1, 3):
-                t_vy(i, o).start()
-            for o in (3, 2, 1):
-                t_vz(i, o).start()
-
-    @pl.when((zlo == 0) & (y != 0))
-    def _():
-        t_gs(1, y).wait_recv()
-        for o in (3, 2, 1):
-            t_gt(o, (zlo + o) % 4).start()
-            t_gz(o, zlo).start()
-
-    for i in CHUNKS:
-        @pl.when((zlo == 0) & (y != 0))
-        def _(i=i):
-            t_vy(i, 1).wait_recv()
-            for o in (3, 2, 1):
-                t_vz(i, o).start()
-
-        @pl.when(zlo != 0)
-        def _(i=i):
-            t_vz(i, 1).wait_recv()
-
-        for o in (2, 1, 3):
-            t_vx(i, o, x).start()
-
-    @pl.when(first)
-    def _():
-        for s in (0, 1):
-            for e in (1, 2, 3):
-                t_rz(s, e, (z - e) % 4).wait_recv()
-            panel_ref[s, x, core, :, n:2 * n] = (rz[0, s] + rz[1, s]) + (rz[2, s] + rz[3, s])
-
-        @pl.when(z >= 2)
-        def _():
-            for e in (1, 2, 3):
-                t_ry(e).wait_recv()
-            rows_ref[0, 0] = rows_ref[0, 0] + ((rz[z, z] + ry[0]) + (ry[1] + ry[2]))
-
-        for o in (3, 2, 1):
-            t_gz(o, zlo).start()
-
-    @pl.when(zlo != 0)
-    def _():
-        t_gt(1, zlo).wait_recv()
-        for o in (1, 2, 3):
-            @pl.when((zlo + o) % 4 != 0)
-            def _(o=o):
-                t_gz(o, zlo).start()
-
-    for s in (0, 1):
-        @pl.when(others & (z != s))
-        def _(s=s):
-            got_fz(s).wait_recv()
-
-        @pl.when(others)
-        def _(s=s):
-            for o in (2, 1, 3):
-                t_fx(s, o, x).start()
-
-        @pl.when(first)
-        def _(s=s):
-            for o in (2, 1, 3):
-                t_fx(s, o, x, n).start()
-    for i in CHUNKS:
-        for o in (1, 2, 3):
-            t_vx(i, o, (x - o) % 4).wait_recv()
-        t_vc(i, core).start()
 
     def band_x(e, lo):
         q = (z + e) % 4
@@ -483,8 +393,108 @@
 
     @pl.when(others)
     def _():
+        for e in (2, 1):
+            combine((z + e) % 4)
+        for s in (0, 1):
+            @pl.when(z != s)
+            def _(s=s):
+                got_fz(s).wait_recv()
+
+            for o in (2, 1, 3):
+                t_fx(s, o, x).start()
+        for e in (3, 0):
+            combine((z + e) % 4)
+
+    @pl.when(first)
+    def _():
+        for q in (2, 3):
+            t_core(q, n).wait_recv()
+            core_sum[q, :, :, n:2 * n] = part[q, :, core, :, n:2 * n] + core_in[q, :, :, n:2 * n]
+            for o in (2, 1, 3):
+                t_x(q, o, n).start()
+
+    @pl.when(first)
+    def _():
+        for i in CHUNKS:
+            for e in (1, 2, 3):
+                t_pz(i, e, (z - e) % 4).wait_recv()
+            lanes = slice(m * i, n)
+            piv[i, x, core, :, lanes] = (pz[0, i, :, lanes] + pz[1, i, :, lanes]) + (
+                pz[2, i, :, lanes] + pz[3, i, :, lanes])
+            for o in (3, 2, 1):
+                t_vz(i, o).start()
+            for o in (2, 1, 3):
+                t_vy(i, o).start()
+
+    @pl.when((zlo == 0) & (y != 0))
+    def _():
+        t_gs(1, y).wait_recv()
+        for o in (3, 2, 1):
+            t_gt(o, (zlo + o) % 4).start()
+            t_gz(o, zlo).start()
+
+    @pl.when(y != 0)
+    def _():
+        band_x(2, 0)
+
+    for i in CHUNKS:
+        @pl.when((y == 0) & (zlo != 0))
+        def _(i=i):
+            t_vz(i, 1).wait_recv()
+            for o in (2, 1, 3):
+                t_vy(i, o).start()
+
+        @pl.when(y != 0)
+        def _(i=i):
+            t_vy(i, 1).wait_recv()
+
+        for o in (2, 1, 3):
+            t_vx(i, o, x).start()
+
+    @pl.when((y == 0) & (zlo != 0))
+    def _():
         for e in (2, 1, 3):
             band_x(e, 0)
+
+    @pl.when(first)
+    def _():
+        for s in (0, 1):
+            for e in (1, 2, 3):
+                t_rz(s, e, (z - e) % 4).wait_recv()
+            panel_ref[s, x, core, :, n:2 * n] = (rz[0, s] + rz[1, s]) + (rz[2, s] + rz[3, s])
+
+        @pl.when(z >= 2)
+        def _():
+            for e in (1, 2, 3):
+                t_ry(e).wait_recv()
+            rows_ref[0, 0] = rows_ref[0, 0] + ((rz[z, z] + ry[0]) + (ry[1] + ry[2]))
+
+        for o in (3, 2, 1):
+            t_gz(o, zlo).start()
+
+    @pl.when(zlo != 0)
+    def _():
+        t_gt(1, zlo).wait_recv()
+        for o in (1, 2, 3):
+            @pl.when((zlo + o) % 4 != 0)
+            def _(o=o):
+                t_gz(o, zlo).start()
+
+    @pl.when(first)
+    def _():
+        for s in (0, 1):
+            for o in (2, 1, 3):
+                t_fx(s, o, x, n).start()
+
+    @pl.when(y != 0)
+    def _():
+        for e in (1, 3):
+            band_x(e, 0)
+
+    for i in CHUNKS:
+        for o in (1, 2, 3):
+            t_vx(i, o, (x - o) % 4).wait_recv()
+        t_vc(i, core).start()
 
     @pl.when(first)
     def _():
@@ -503,14 +513,20 @@
             for v in (2, 1, 3):
                 t_gy(l, v, y).start()
 
-    def panel_core():
-        for mine, lo in ((others, 0), (first, n)):
-            @pl.when(mine)
-            def _(lo=lo):
-                for s in (0, 1):
-                    for o in (1, 2, 3):
-                        t_fx(s, o, (x - o) % 4, lo).wait_recv()
-                    t_fc(s, core, lo).start()
+    def panel_core(lo):
+        for s in (0, 1):
+            for o in (1, 2, 3):
+                t_fx(s, o, (x - o) % 4, lo).wait_recv()
+            t_fc(s, core, lo).start()
+
+    @pl.when(others)
+    def _():
+        panel_core(0)
+
+    def late_panel():
+        @pl.when(first)
+        def _():
+            panel_core(n)
 
     def step(k, _):
         for i in CHUNKS:
@@ -518,7 +534,7 @@
             def _(i=i):
                 t_vc(i, other).wait_recv()
         factor_chunk(k, piv.at[k], inv_ref, held, done, gathered)
-        for kk, work in enumerate((spread, panel_core)):
+        for kk, work in enumerate((spread, late_panel)):
             @pl.when(k == kk)
             def _(work=work):
                 work()
@@ -533,6 +549,17 @@
         def _(lo=lo):
             for s in (0, 1):
                 t_fc(s, other, lo).wait_recv()
+
+    for lo, hi in ((0, 256), (256, 512)):
+        inv = split(inv_ref[lo:hi, 0:hi])
+        for j in range(4):
+            to = slice(256 * j, 256 * (j + 1))
+            given = panel_ref[:, :, :, :, to].reshape(n, 256)
+            uh_ref[lo:hi, to], ul_ref[lo:hi, to] = split(dot3(inv, split(given[0:hi])))
+        for j in range(2):
+            to = slice(256 * j, 256 * (j + 1))
+            given = rows_ref[2 * j:2 * j + 2].reshape(256, n)
+            vh_ref[to, lo:hi], vl_ref[to, lo:hi] = split(dot3(split(given[:, 0:hi]), inv, trans=True))
 
     def share_of(lo):
         for e in (1, 2, 3):
@@ -596,8 +623,12 @@
     def _():
         for o in (1, 2, 3):
             t_gt(o, (zlo + o) % 4).wait_send()
-            for i in CHUNKS:
-                t_vz(i, o).wait_send()
+
+    @pl.when(y == 0)
+    def _():
+        for i in CHUNKS:
+            for o in (1, 2, 3):
+                t_vy(i, o).wait_send()
 
     @pl.when((row != 0) & (z < 2))
     def _():
@@ -611,7 +642,7 @@
             for i in CHUNKS:
                 t_px(i, o).wait_send()
                 t_pz(i, o, z).wait_send()
-                t_vy(i, o).wait_send()
+                t_vz(i, o).wait_send()
             for s in range(4):
                 t_rx(s, o).wait_send()
                 if s < 2:
@@ -634,14 +665,14 @@
         schur_kernel,
         name="schur",
         out_shape=(
-            jax.ShapeDtypeStruct((512, 512), F32),
-            jax.ShapeDtypeStruct((2, 4, 2, 32, 1024), F32),
-            jax.ShapeDtypeStruct((4, 4, 32, 512), F32),
+            jax.ShapeDtypeStruct((512, 1024), BF16), jax.ShapeDtypeStruct((512, 1024), BF16),
+            jax.ShapeDtypeStruct((512, 512), BF16), jax.ShapeDtypeStruct((512, 512), BF16),
             jax.ShapeDtypeStruct((32, 1024), F32),
         ),
         in_specs=[spec, spec, pl.BlockSpec(memory_space=pltpu.HBM)],
-        out_specs=(spec,) * 4,
+        out_specs=(spec,) * 5,
         scratch_shapes=[
+            VM((512, 512), F32), VM((2, 4, 2, 32, 1024), F32), VM((4, 4, 32, 512), F32),
             VM((16, 32, 1024), BF16), dma(()),
             VM((4, 4, 2, 32, 1024), F32), VM((4, 4, 2, 16, 512), F32), VM((4, 4, 2, 32, 512), F32),
             VM((4, 4, 32, 1024), F32), VM((4, 4, 32, 1024), F32),
@@ -675,22 +706,10 @@
     return mm(ah, bh) + (mm(ah, bl) + mm(al, bh))
 
 
-def apply_kernel(inv_ref, panel_ref, rows_ref, hess_ref, share_ref, out_ref, uh, ul, vh, vl):
+def apply_kernel(uh, ul, vh, vl, hess_ref, share_ref, out_ref):
     row = lax.axis_index("row")
     col = lax.axis_index("col")
     at = pl.program_id(0)
-
-    @pl.when(at == 0)
-    def _():
-        for lo, hi in ((0, 256), (256, 512)):
-            inv = split(inv_ref[lo:hi, 0:hi])
-            for j in range(4):
-                part = slice(256 * j, 256 * (j + 1))
-                uh[lo:hi, part], ul[lo:hi, part] = split(dot3(inv, split(panel_ref[0:hi, part])))
-            for j in range(2):
-                part = slice(256 * j, 256 * (j + 1))
-                vh[part, lo:hi], vl[part, lo:hi] = split(dot3(split(rows_ref[part, 0:hi]), inv, trans=True))
-
     rows = pl.ds(pl.multiple_of(at * 128, 128), 128)
     update = dot3((vh[rows, :], vl[rows, :]), (uh[...], ul[...]))
     lane = lax.broadcasted_iota(jnp.int32, (1, 1024), 1)
@@ -701,7 +720,7 @@
         out_ref[q] = jnp.where(keep, schur - update[32 * q:32 * (q + 1), :], 0.0)
 
 
-def apply(inv, panel, rows, hessian, share):
+def apply(uh, ul, vh, vl, hessian, share):
     whole = lambda *s: pl.BlockSpec(s, lambda i: (0,) * len(s))
     return pl.pallas_call(
         apply_kernel,
@@ -709,21 +728,20 @@
         grid=(4,),
         out_shape=jax.ShapeDtypeStruct((16, 32, 1024), F32),
         in_specs=[
-            whole(512, 512), whole(512, 1024), whole(512, 512),
+            whole(512, 1024), whole(512, 1024), whole(512, 512), whole(512, 512),
             pl.BlockSpec((4, 32, 1024), lambda i: (i, 0, 0)), whole(32, 1024),
         ],
         out_specs=pl.BlockSpec((4, 32, 1024), lambda i: (i, 0, 0)),
-        scratch_shapes=[VM((512, 1024), BF16), VM((512, 1024), BF16), VM((512, 512), BF16), VM((512, 512), BF16)],
         compiler_params=pltpu.CompilerParams(
             dimension_semantics=("arbitrary",), vmem_limit_bytes=40 * 2**20
         ),
-    )(inv, panel, rows, hessian, share)
+    )(uh, ul, vh, vl, hessian, share)
 
 
 def local(coupling, kinv, counts, granules, hessian, reg):
     embedded, diag = embed(coupling[0], kinv[0], counts, granules, reg)
-    inv, panel, rows, share = schur(embedded, diag, hessian)
-    return apply(inv, panel.reshape(512, 1024), rows.reshape(512, 512), hessian, share)
+    uh, ul, vh, vl, share = schur(embedded, diag, hessian)
+    return apply(uh, ul, vh, vl, hessian, share)
 
 
 def solution(mesh):

time: 110 us -> 112 us (1.018)
  Pallas kernels: 108 us -> 110 us
    pallas_call x1, Pallas kernels: 99.8 us -> 104 us  [schur(): pl.pallas_call(schur_kernel, name='schur', out_shape=(jax.ShapeDtypeStruc...]
    pallas_call x1, Pallas kernels: 5.49 us -> 3.4 us  [apply(): pl.pallas_call(apply_kernel, name='apply', grid=(4,), out_shape=jax.Shape...]
where the time goes in v3:
time: 112 us; the launch traced here: 111 us
  Pallas kernels  110 us (98%)
    pallas_call x1, Pallas kernels, schur(): pl.pallas_call(schur_kernel, name='schur', out_shape=(jax.ShapeDtypeStruc...  104 us
    pallas_call x1, Pallas kernels, apply(): pl.pallas_call(apply_kernel, name='apply', grid=(4,), out_shape=jax.Shape...  3.4 us
    pallas_call x1, Pallas kernels, embed(): pl.pallas_call(embed_kernel, name='embed', out_shape=(jax.ShapeDtypeStruc...  2.77 us

profile of v3, /device:TPU:160, one launch (start us, length us, event | category | flops | bytes accessed | tf_op | source)
XLA Modules:
  0.0 111.5 jit_solution(6359530743724923708)
XLA Ops:
  0.7 0.0 copy-start.1
  0.7 0.6 copy-done.1
  1.3 0.0 copy-start
  1.3 2.8 %embed.1 = (bf16[2,1024,512]{2,1,0:T(8,128)(2,1)S(1)}, f32[32,1024]{1,0:T(8,128)S(1)}) custom-call(s32[1]{0:T(128)S(6)} %copy.7.counts_ref, s32[1,8]{1,0:T(1,128)S(1)} %copy-done.1, f32[1,1024]{1,0:T(1,128)} %bitcast.5, bf16[1024,512]{1,0:T(8,128)(2,1)} %bitcast.3, bf16[512,512]{1,0:T(8,128)(2,1)} %bitcast.4), custom_call_target="tpu_custom_call" | custom-call | tf_op jit(solution)/shard_map/embed/pallas_call | solution.py:54
  4.1 104.0 %schur.1 = (bf16[512,1024]{1,0:T(8,128)(2,1)S(1)}, bf16[512,1024]{1,0:T(8,128)(2,1)S(1)}, bf16[512,512]{1,0:T(8,128)(2,1)S(1)}, bf16[512,512]{1,0:T(8,128)(2,1)S(1)}, f32[32,1024]{1,0:T(8,128)S(1)}) custom-call(bf16[2,1024,512]{2,1,0:T(8,128)(2,1)S(1)} %get-tuple-element.12.emb_ref, f32[32,1024]{1,0:T(8,128)S(1)} %get-tuple-element.13.diag_ref, ...), custom_call_target="tpu_custom_call" | custom-call | tf_op jit(solution)/shard_map/schur/pallas_call | solution.py:664
  108.1 0.0 copy-done
  108.1 3.4 %apply.1 = f32[16,32,1024]{2,1,0:T(8,128)} custom-call(bf16[512,1024]{1,0:T(8,128)(2,1)S(1)} %get-tuple-element.14.uh, bf16[512,1024]{1,0:T(8,128)(2,1)S(1)} %get-tuple-element.15.ul, bf16[512,512]{1,0:T(8,128)(2,1)S(1)} %get-tuple-element.16.vh, bf16[512,512]{1,0:T(8,128)(2,1)S(1)} %get-tuple-element.17.vl, bf16[16,32,1024]{2,1,0:T(8,128)(2,1)S(1)} %copy-done, ...), custom_call_target="tpu_custom_call" | custom-call | tf_op jit(solution)/shard_map/apply/pallas_call | solution.py:725
Async XLA Ops:
  0.7 0.7 copy-start.1
  1.3 106.8 %copy-start = (bf16[16,32,1024]{2,1,0:T(8,128)(2,1)S(1)}, bf16[16,32,1024]{2,1,0:T(8,128)(2,1)}, u32[]{:S(2)}) copy-start(bf16[16,32,1024]{2,1,0:T(8,128)(2,1)} %hess_ref.1) | copy-start | bytes 3145732

commit v4 on v2

--- a/solution.py
+++ b/solution.py
@@ -142,8 +142,8 @@
 
 def schur_kernel(
     emb_ref, diag_ref, hess_hbm,
-    inv_ref, panel_ref, rows_ref, share_ref,
-    hess_ref, load,
+    uh_ref, ul_ref, vh_ref, vl_ref, share_ref,
+    inv_ref, panel_ref, rows_ref, hess_ref, load,
     part, dp, dr, core_in, core_sum, x_in, x_sum, z_in, piv,
     pc_in, pc_sum, px_in, pz, rc_in, rc_sum, rx_in, rz, ry, spare, held, done, gathered,
     s_core, r_core, s_x, r_x, s_z, r_z,
@@ -376,16 +376,25 @@
             def _(e=e):
                 t_ry(e).start()
 
-    def combine(q, _):
+    def combine(q):
         t_core(q).wait_recv()
         core_sum[q] = part[q, :, core] + core_in[q]
         for o in (2, 1, 3):
             t_x(q, o).start()
-        return 0
 
     @pl.when(others)
     def _():
-        lax.fori_loop(0, 4, combine, 0)
+        for q in (0, 1):
+            combine(q)
+        for s in (0, 1):
+            @pl.when(z != s)
+            def _(s=s):
+                got_fz(s).wait_recv()
+
+            for o in (2, 1, 3):
+                t_fx(s, o, x).start()
+        for q in (2, 3):
+            combine(q)
 
     @pl.when(first)
     def _():
@@ -453,20 +462,12 @@
             def _(o=o):
                 t_gz(o, zlo).start()
 
-    for s in (0, 1):
-        @pl.when(others & (z != s))
-        def _(s=s):
-            got_fz(s).wait_recv()
-
-        @pl.when(others)
-        def _(s=s):
-            for o in (2, 1, 3):
-                t_fx(s, o, x).start()
-
-        @pl.when(first)
-        def _(s=s):
+    @pl.when(first)
+    def _():
+        for s in (0, 1):
             for o in (2, 1, 3):
                 t_fx(s, o, x, n).start()
+
     for i in CHUNKS:
         for o in (1, 2, 3):
             t_vx(i, o, (x - o) % 4).wait_recv()
@@ -534,6 +535,17 @@
             for s in (0, 1):
                 t_fc(s, other, lo).wait_recv()
 
+    for lo, hi in ((0, 256), (256, 512)):
+        inv = split(inv_ref[lo:hi, 0:hi])
+        for j in range(4):
+            to = slice(256 * j, 256 * (j + 1))
+            given = panel_ref[:, :, :, :, to].reshape(n, 256)
+            uh_ref[lo:hi, to], ul_ref[lo:hi, to] = split(dot3(inv, split(given[0:hi])))
+        for j in range(2):
+            to = slice(256 * j, 256 * (j + 1))
+            given = rows_ref[2 * j:2 * j + 2].reshape(256, n)
+            vh_ref[to, lo:hi], vl_ref[to, lo:hi] = split(dot3(split(given[:, 0:hi]), inv, trans=True))
+
     def share_of(lo):
         for e in (1, 2, 3):
             t_z(e, lo).wait_recv()
@@ -634,14 +646,14 @@
         schur_kernel,
         name="schur",
         out_shape=(
-            jax.ShapeDtypeStruct((512, 512), F32),
-            jax.ShapeDtypeStruct((2, 4, 2, 32, 1024), F32),
-            jax.ShapeDtypeStruct((4, 4, 32, 512), F32),
+            jax.ShapeDtypeStruct((512, 1024), BF16), jax.ShapeDtypeStruct((512, 1024), BF16),
+            jax.ShapeDtypeStruct((512, 512), BF16), jax.ShapeDtypeStruct((512, 512), BF16),
             jax.ShapeDtypeStruct((32, 1024), F32),
         ),
         in_specs=[spec, spec, pl.BlockSpec(memory_space=pltpu.HBM)],
-        out_specs=(spec,) * 4,
+        out_specs=(spec,) * 5,
         scratch_shapes=[
+            VM((512, 512), F32), VM((2, 4, 2, 32, 1024), F32), VM((4, 4, 32, 512), F32),
             VM((16, 32, 1024), BF16), dma(()),
             VM((4, 4, 2, 32, 1024), F32), VM((4, 4, 2, 16, 512), F32), VM((4, 4, 2, 32, 512), F32),
             VM((4, 4, 32, 1024), F32), VM((4, 4, 32, 1024), F32),
@@ -675,22 +687,10 @@
     return mm(ah, bh) + (mm(ah, bl) + mm(al, bh))
 
 
-def apply_kernel(inv_ref, panel_ref, rows_ref, hess_ref, share_ref, out_ref, uh, ul, vh, vl):
+def apply_kernel(uh, ul, vh, vl, hess_ref, share_ref, out_ref):
     row = lax.axis_index("row")
     col = lax.axis_index("col")
     at = pl.program_id(0)
-
-    @pl.when(at == 0)
-    def _():
-        for lo, hi in ((0, 256), (256, 512)):
-            inv = split(inv_ref[lo:hi, 0:hi])
-            for j in range(4):
-                part = slice(256 * j, 256 * (j + 1))
-                uh[lo:hi, part], ul[lo:hi, part] = split(dot3(inv, split(panel_ref[0:hi, part])))
-            for j in range(2):
-                part = slice(256 * j, 256 * (j + 1))
-                vh[part, lo:hi], vl[part, lo:hi] = split(dot3(split(rows_ref[part, 0:hi]), inv, trans=True))
-
     rows = pl.ds(pl.multiple_of(at * 128, 128), 128)
     update = dot3((vh[rows, :], vl[rows, :]), (uh[...], ul[...]))
     lane = lax.broadcasted_iota(jnp.int32, (1, 1024), 1)
@@ -701,7 +701,7 @@
         out_ref[q] = jnp.where(keep, schur - update[32 * q:32 * (q + 1), :], 0.0)
 
 
-def apply(inv, panel, rows, hessian, share):
+def apply(uh, ul, vh, vl, hessian, share):
     whole = lambda *s: pl.BlockSpec(s, lambda i: (0,) * len(s))
     return pl.pallas_call(
         apply_kernel,
@@ -709,21 +709,20 @@
         grid=(4,),
         out_shape=jax.ShapeDtypeStruct((16, 32, 1024), F32),
         in_specs=[
-            whole(512, 512), whole(512, 1024), whole(512, 512),
+            whole(512, 1024), whole(512, 1024), whole(512, 512), whole(512, 512),
             pl.BlockSpec((4, 32, 1024), lambda i: (i, 0, 0)), whole(32, 1024),
         ],
         out_specs=pl.BlockSpec((4, 32, 1024), lambda i: (i, 0, 0)),
-        scratch_shapes=[VM((512, 1024), BF16), VM((512, 1024), BF16), VM((512, 512), BF16), VM((512, 512), BF16)],
         compiler_params=pltpu.CompilerParams(
             dimension_semantics=("arbitrary",), vmem_limit_bytes=40 * 2**20
         ),
-    )(inv, panel, rows, hessian, share)
+    )(uh, ul, vh, vl, hessian, share)
 
 
 def local(coupling, kinv, counts, granules, hessian, reg):
     embedded, diag = embed(coupling[0], kinv[0], counts, granules, reg)
-    inv, panel, rows, share = schur(embedded, diag, hessian)
-    return apply(inv, panel.reshape(512, 1024), rows.reshape(512, 512), hessian, share)
+    uh, ul, vh, vl, share = schur(embedded, diag, hessian)
+    return apply(uh, ul, vh, vl, hessian, share)
 
 
 def solution(mesh):

time: 110 us -> 106 us (0.964)
  the two profiles are of different devices: /device:TPU:160 before, /device:TPU:193 now
where the time goes in v4:
time: 106 us
  Pallas kernels  104 us (98%)
    pallas_call x1, Pallas kernels, schur(): pl.pallas_call(schur_kernel, name='schur', out_shape=(jax.ShapeDtypeStruc...  98.3 us
    pallas_call x1, Pallas kernels, apply(): pl.pallas_call(apply_kernel, name='apply', grid=(4,), out_shape=jax.Shape...  3.4 us
    pallas_call x1, Pallas kernels, embed(): pl.pallas_call(embed_kernel, name='embed', out_shape=(jax.ShapeDtypeStruc...  2.77 us

profile of v4, /device:TPU:193, one launch (start us, length us, event | category | flops | bytes accessed | tf_op | source)
XLA Modules:
  0.0 105.8 jit_solution(13762340497843422191)
XLA Ops:
  0.7 0.0 copy-start.1
  0.7 0.6 copy-done.1
  1.3 0.0 copy-start
  1.3 2.8 %embed.1 = (bf16[2,1024,512]{2,1,0:T(8,128)(2,1)S(1)}, f32[32,1024]{1,0:T(8,128)S(1)}) custom-call(s32[1]{0:T(128)S(6)} %copy.7.counts_ref, s32[1,8]{1,0:T(1,128)S(1)} %copy-done.1, f32[1,1024]{1,0:T(1,128)} %bitcast.5, bf16[1024,512]{1,0:T(8,128)(2,1)} %bitcast.3, bf16[512,512]{1,0:T(8,128)(2,1)} %bitcast.4), custom_call_target="tpu_custom_call" | custom-call | tf_op jit(solution)/shard_map/embed/pallas_call | solution.py:54
  4.1 98.3 %schur.1 = (bf16[512,1024]{1,0:T(8,128)(2,1)S(1)}, bf16[512,1024]{1,0:T(8,128)(2,1)S(1)}, bf16[512,512]{1,0:T(8,128)(2,1)S(1)}, bf16[512,512]{1,0:T(8,128)(2,1)S(1)}, f32[32,1024]{1,0:T(8,128)S(1)}) custom-call(bf16[2,1024,512]{2,1,0:T(8,128)(2,1)S(1)} %get-tuple-element.12.emb_ref, f32[32,1024]{1,0:T(8,128)S(1)} %get-tuple-element.13.diag_ref, ...), custom_call_target="tpu_custom_call" | custom-call | tf_op jit(solution)/shard_map/schur/pallas_call | solution.py:645
  102.4 0.0 copy-done
  102.4 3.4 %apply.1 = f32[16,32,1024]{2,1,0:T(8,128)} custom-call(bf16[512,1024]{1,0:T(8,128)(2,1)S(1)} %get-tuple-element.14.uh, bf16[512,1024]{1,0:T(8,128)(2,1)S(1)} %get-tuple-element.15.ul, bf16[512,512]{1,0:T(8,128)(2,1)S(1)} %get-tuple-element.16.vh, bf16[512,512]{1,0:T(8,128)(2,1)S(1)} %get-tuple-element.17.vl, bf16[16,32,1024]{2,1,0:T(8,128)(2,1)S(1)} %copy-done, ...), custom_call_target="tpu_custom_call" | custom-call | tf_op jit(solution)/shard_map/apply/pallas_call | solution.py:706
Async XLA Ops:
  0.7 0.7 copy-start.1
  1.3 101.1 %copy-start = (bf16[16,32,1024]{2,1,0:T(8,128)(2,1)S(1)}, bf16[16,32,1024]{2,1,0:T(8,128)(2,1)}, u32[]{:S(2)}) copy-start(bf16[16,32,1024]{2,1,0:T(8,128)(2,1)} %hess_ref.1) | copy-start | bytes 3145732
